TPU v7x, 32 devices: a whole 2x2x4 slice. The times are simulated.
32 devices in a mesh: grp: 2 (over y), occ: 4 (over z), aux: 2 (over x), vir: 2 (over core).
Axes of the slice: x: 2, y: 2, z: 4, core: 2. Of those that a mesh axis runs over, the one named last changes fastest.
Arguments:
- integrals: bfloat16 [4, 1024, 8, 1280], P('occ', 'aux', 'grp', 'vir'), parts along dimension 2, may hold values from -0.59765625 to 0.59765625
- occ_energy: float32 [8], P('grp'), parts along dimension 0, may hold values from -1.5 to -0.3
- vir_energy: float32 [2560], P('grp'), parts along dimension 0, may hold values from 0.2 to 3
- round_owner: int32 [4], P('grp'), parts along dimension 0, may hold values from 0 to 3, as said below
Outputs:
- gamma_field: float32 [8, 1024, 4, 1280], P('grp', 'aux', 'occ', 'vir'), parts along dimension 0
There are 2 independent parts, one for each index of `grp`. A program takes and returns all parts, laid end to end along the dimension named above; each array names one. Nothing has to cross between parts.
Inputs may be any that keep to these rules, and one draw needn't show every extreme that they name: `round_owner`: the 2 owners are distinct.
All inputs are finite; a program needn't handle non-finite values.
Results may differ from a plain program's by a relative error of at most 0.0085.
Values may be sent and summed in bfloat16 or wider, within the bound.
No kernel may reach another device: no remote copies, remote signals or barrier semaphores. Data moves between devices by JAX's collectives and lax.ppermute only.
A program may use at most 64 MiB of HBM per device.

v0:
```python
import jax
import jax.numpy as jnp
from jax import lax
from jax.sharding import PartitionSpec as P

ROUNDS = 2


def from_root(value, axis, root):
    mine = lax.axis_index(axis) == root
    return lax.psum(jnp.where(mine, value, jnp.zeros_like(value)), axis)


def local(integrals, occ_energy, vir_energy, round_owner):
    regrouped = lax.all_to_all(integrals, "occ", split_axis=2, concat_axis=0, tiled=True)
    occ_width = regrouped.shape[2]
    vir_width = regrouped.shape[3]
    energy_i = lax.dynamic_slice_in_dim(occ_energy, lax.axis_index("occ") * occ_width, occ_width)
    energy_a = lax.dynamic_slice_in_dim(vir_energy, lax.axis_index("vir") * vir_width, vir_width)
    gamma_total = jnp.zeros(regrouped.shape, jnp.float32)
    for turn_index in range(ROUNDS):
        owner = round_owner[turn_index]
        owner_half = from_root(regrouped, "occ", owner)
        owner_whole = lax.all_gather(owner_half, "vir", axis=3, tiled=True)
        energy_j = lax.dynamic_slice_in_dim(occ_energy, owner * occ_width, occ_width)
        partial_value = jnp.einsum(
            "sria,srjb->ijab", regrouped, owner_whole, preferred_element_type=jnp.float32
        )
        base = energy_i[:, None, None] + energy_j[None, :, None] - energy_a[None, None, :]
        pair_block = lax.psum(partial_value.astype(jnp.bfloat16), "aux").astype(jnp.float32)
        amplitude = (pair_block / (base[..., None] - vir_energy)).astype(jnp.bfloat16)
        gamma_total = gamma_total + jnp.einsum(
            "ijab,srjb->sria", amplitude, owner_whole, preferred_element_type=jnp.float32
        )
    return gamma_total


def solution(mesh):
    placed = (P("occ", "aux", "grp", "vir"), P("grp"), P("grp"), P("grp"))
    return jax.shard_map(
        local, mesh=mesh, in_specs=placed, out_specs=P("grp", "aux", "occ", "vir"), check_vma=False
    )
```

profile of v0, /device:TPU:0, one launch (start us, length us, event | category | flops | bytes accessed | tf_op | source)
XLA Modules:
  0.0 432.3 jit_solution(8235440638298763735)
XLA Ops:
  6.5 3.6 copy.11
  10.1 0.0 copy-start.2
  10.1 6.4 %all-to-all-start = ((bf16[1,512,4,640]{3,1,0,2:T(8,128)(2,1)}), bf16[1,512,4,640]{3,1,0,2:T(8,128)(2,1)S(1)}, u32[]{:S(2)}, u32[]{:S(2)}) async-start(bf16[1,512,4,640]{3,1,0,2:T(8,128)(2,1)} %copy.11), calls=%async_computation | async-start | bytes 5242880 | tf_op jit(solution)/shard_map/all_to_all | solution.py:15
  16.5 0.0 all-reduce.5.cloned.1.call-start
  16.5 0.0 copy-done.2
  16.6 0.7 fusion.41
  18.5 57.4 %all-to-all-done = bf16[1,512,4,640]{3,1,0,2:T(8,128)(2,1)S(1)} async-done(((bf16[1,512,4,640]{3,1,0,2:T(8,128)(2,1)}), bf16[1,512,4,640]{3,1,0,2:T(8,128)(2,1)S(1)}, u32[]{:S(2)}, u32[]{:S(2)}) %all-to-all-start) | async-done | bytes 2621472 | tf_op jit(solution)/shard_map/all_to_all | solution.py:15
  76.0 2.8 fusion.28
  78.8 0.0 all-reduce.5.cloned.1.call-update
  78.8 0.0 all-gather.3.cloned.1.call-start
  78.8 188.5 %all-reduce.5.cloned.1.call-done = (bf16[4,512,1,640]{3,1,0,2:T(8,128)(2,1)}, bf16[4,512,1,640]{3,1,0,2:T(8,128)(2,1)}) async-done(((bf16[4,512,1,640]{3,1,0,2:T(8,128)(2,1)}, bf16[4,512,1,640]{3,1,0,2:T(8,128)(2,1)}), (bf16[4,512,1,640]{3,1,0,2:T(8,128)(2,1)}, bf16[4,512,1,640]{3,1,0,2:T(8,128)(2,1)})) %all-reduce.5.cloned.1.call-update) | async-done | bytes 5242896 | tf_op jit(solution)/shard_map/psum | solution.py:11
  267.3 0.0 all-gather.3.cloned.1.call-update
  267.4 0.0 all-gather.5.cloned.1.call-start
  267.4 0.7 all-gather.5.cloned.1.call-update
  268.1 0.0 all-reduce.7.cloned.1.call-start
  268.1 14.9 %all-gather.3.cloned.1.call-done = bf16[4,512,1,1280]{3,1,0,2:T(8,128)(2,1)} async-done(((bf16[4,512,1,640]{3,1,0,2:T(8,128)(2,1)}), bf16[4,512,1,1280]{3,1,0,2:T(8,128)(2,1)}) %all-gather.3.cloned.1.call-update) | async-done | bytes 5242896 | tf_op jit(solution)/shard_map/all_gather | solution.py:24
  283.0 8.0 %fusion.20 = bf16[1,1,640,1280]{2,3,0,1:T(8,128)(2,1)} fusion(bf16[4,512,1,1280]{3,1,0,2:T(8,128)(2,1)} %all-gather.3.cloned.1.call-done, bf16[1,512,4,640]{3,1,0,2:T(8,128)(2,1)S(1)} %all-to-all-done), kind=kOutput, calls=%fused_computation.15 | convolution fusion | flops 3356262400 | bytes 9502720 | tf_op jit(solution)/shard_map/sria,srjb->ijab/dot_general | solution.py:26
  291.0 9.9 %all-gather.5.cloned.1.call-done = bf16[4,512,1,1280]{3,1,0,2:T(8,128)(2,1)} async-done(((bf16[4,512,1,640]{3,1,0,2:T(8,128)(2,1)}), bf16[4,512,1,1280]{3,1,0,2:T(8,128)(2,1)}) %all-gather.5.cloned.1.call-update) | async-done | bytes 5242896 | tf_op jit(solution)/shard_map/all_gather | solution.py:24
  300.9 8.0 %fusion.23 = bf16[1,1,640,1280]{2,3,0,1:T(8,128)(2,1)} fusion(bf16[4,512,1,1280]{3,1,0,2:T(8,128)(2,1)} %all-gather.5.cloned.1.call-done, bf16[1,512,4,640]{3,1,0,2:T(8,128)(2,1)S(1)} %all-to-all-done), kind=kOutput, calls=%fused_computation.16 | convolution fusion | flops 3356262400 | bytes 9502720 | tf_op jit(solution)/shard_map/sria,srjb->ijab/dot_general | solution.py:26
  308.8 0.0 copy-start
  308.9 0.0 copy-start.1
  308.9 0.0 all-reduce.7.cloned.1.call-update
  312.8 0.0 copy-done
  312.9 0.7 fusion.40
  316.0 0.0 copy-done.1
  316.0 0.1 dynamic-slice_subtract_fusion.1
  316.1 82.9 %all-reduce.7.cloned.1.call-done = (bf16[1,1,640,1280]{2,3,0,1:T(8,128)(2,1)}, bf16[1,1,640,1280]{2,3,0,1:T(8,128)(2,1)}) async-done(((bf16[1,1,640,1280]{2,3,0,1:T(8,128)(2,1)}, bf16[1,1,640,1280]{2,3,0,1:T(8,128)(2,1)}), (bf16[1,1,640,1280]{2,3,0,1:T(8,128)(2,1)}, bf16[1,1,640,1280]{2,3,0,1:T(8,128)(2,1)})) %all-reduce.7.cloned.1.call-update) | async-done | bytes 3276816 | tf_op jit(solution)/shard_map/psum | solution.py:30
  399.0 0.0 copy-start.3
  399.0 7.2 %fusion = f32[4,512,640]{2,1,0:T(8,128)S(1)} fusion(bf16[4,512,1,1280]{3,1,0,2:T(8,128)(2,1)} %all-gather.5.cloned.1.call-done, bf16[1,1,640,1280]{2,3,0,1:T(8,128)(2,1)} %get-tuple-element.7, f32[640]{0:T(1024)S(1)} %get-tuple-element.12, f32[1280]{0:T(1024)S(1)} %copy-done.1), kind=kOutput, calls=%fused_computation | convolution fusion | flops 3358720000 | bytes 12131840 | tf_op jit(solution)/shard_map/ijab,srjb->sria/dot_general | solution.py:32
  406.2 0.0 copy-done.3
  406.2 9.3 %add_bitcast_fusion = f32[4,512,1,640]{3,1,0,2:T(8,128)} fusion(f32[4,512,640]{2,1,0:T(8,128)S(1)} %fusion, bf16[4,512,1,1280]{3,1,0,2:T(8,128)(2,1)} %all-gather.3.cloned.1.call-done, bf16[1,1,640,1280]{2,3,0,1:T(8,128)(2,1)S(1)} %copy-done.3, f32[1280]{0:T(1024)S(1)} %copy-done.1, f32[640]{0:T(1024)S(1)} %get-tuple-element.11), kind=kOutput, calls=%fused_computation.8 | convolution fusion | flops 3360030720 | bytes 17374720 | tf_op jit(solution)/shard_map/ijab,srjb->sria/dot_general | solution.py:32
  415.5 10.2 %copy.16 = f32[4,512,1,640]{3,2,1,0:T(1,128)} copy(f32[4,512,1,640]{3,1,0,2:T(8,128)} %add_bitcast_fusion) | data formatting | bytes 10485760 | tf_op jit(solution)/shard_map/add | solution.py:32
Async XLA Ops:
  10.1 6.5 %copy-start.2 = (s32[2]{0:T(128)S(1)}, s32[2]{0:T(128)}, u32[]{:S(2)}) copy-start(s32[2]{0:T(128)} %param.7) | copy-start | bytes 28
  10.1 65.9 %all-to-all-start = ((bf16[1,512,4,640]{3,1,0,2:T(8,128)(2,1)}), bf16[1,512,4,640]{3,1,0,2:T(8,128)(2,1)S(1)}, u32[]{:S(2)}, u32[]{:S(2)}) async-start(bf16[1,512,4,640]{3,1,0,2:T(8,128)(2,1)} %copy.11), calls=%async_computation | async-start | bytes 5242880 | tf_op jit(solution)/shard_map/all_to_all | solution.py:15
  16.5 250.8 %all-reduce.5.cloned.1.call-start = ((), (), s32[]{:S(2)}) async-start(), calls=%async_computation.3 | async-start | bytes 10485760 | tf_op jit(solution)/shard_map/psum | solution.py:11
  78.8 204.2 %all-gather.3.cloned.1.call-start = ((), (), s32[]{:S(2)}) async-start(), calls=%async_computation.1 | async-start | bytes 7864320 | tf_op jit(solution)/shard_map/all_gather | solution.py:24
  267.4 33.5 %all-gather.5.cloned.1.call-start = ((), (), s32[]{:S(2)}) async-start(), calls=%async_computation.2 | async-start | bytes 7864320 | tf_op jit(solution)/shard_map/all_gather | solution.py:24
  268.1 130.9 %all-reduce.7.cloned.1.call-start = ((), (), s32[]{:S(2)}) async-start(), calls=%async_computation.4 | async-start | bytes 6553600 | tf_op jit(solution)/shard_map/psum | solution.py:30
  308.8 4.0 copy-start
  308.9 7.1 %copy-start.1 = (f32[1280]{0:T(1024)S(1)}, f32[1280]{0:T(1024)}, u32[]{:S(2)}) copy-start(f32[1280]{0:T(1024)} %param.6) | copy-start | bytes 15364
  399.0 7.2 %copy-start.3 = (bf16[1,1,640,1280]{2,3,0,1:T(8,128)(2,1)S(1)}, bf16[1,1,640,1280]{2,3,0,1:T(8,128)(2,1)}, u32[]{:S(2)}) copy-start(bf16[1,1,640,1280]{2,3,0,1:T(8,128)(2,1)} %get-tuple-element.8) | copy-start | bytes 4915204
Sparse Core Ops, SparseCore 0:
  78.9 188.3 all-reduce.4
  268.9 14.0 all-gather.2
  284.6 16.2 all-gather.4
  309.0 89.9 all-reduce.6
where the time goes:
time: 433 us; the launch traced here: 432 us
  waiting for transfers between devices  354 us (82%)
  matrix products  32.4 us (7%)
  between operations  20.9 us (5%)
  local copies, waits for them, and re-layouts  15.1 us (3%)
  starting transfers between devices  6.57 us (2%)
    psum x1, waiting for transfers between devices, from_root(): return lax.psum(jnp.where(mine, value, jnp.zeros_like(value)), axis)  188 us
    psum x1, waiting for transfers between devices, local(): lax.psum(partial_value.astype(jnp.bfloat16), 'aux').astype(jnp.float32)  82.9 us
    all_to_all x1, waiting for transfers between devices, local(): lax.all_to_all(integrals, 'occ', split_axis=2, concat_axis=0, tiled=True)  57.4 us
    all_gather x2, waiting for transfers between devices, local(): owner_whole = lax.all_gather(owner_half, 'vir', axis=3, tiled=True)  24.8 us
    dot_general x2, matrix products, local(): jnp.einsum('ijab,srjb->sria', amplitude, owner_whole, preferred_element_t...  16.5 us
    dot_general x2, matrix products, local(): jnp.einsum('sria,srjb->ijab', regrouped, owner_whole, preferred_element_t...  15.9 us
    add x1, local copies, waits for them, and re-layouts, local(): gamma_total + jnp.einsum('ijab,srjb->sria', amplitude, owner_whole, prefe...  10.2 us
  transfers between devices with their start and end apart: 5, of which 5 were waited for; matrix products, arithmetic and copies ran while one was open for 2% of the time, Pallas kernels for 0%

commit v1 on v0

--- a/solution.py
+++ b/solution.py
@@ -12,7 +12,9 @@
 
 
 def local(integrals, occ_energy, vir_energy, round_owner):
-    regrouped = lax.all_to_all(integrals, "occ", split_axis=2, concat_axis=0, tiled=True)
+    cells = jnp.split(integrals, lax.axis_size("occ"), axis=2)
+    received = lax.all_to_all(jnp.stack(cells), "occ", 0, 0)
+    regrouped = jnp.concatenate(received, axis=0)
     occ_width = regrouped.shape[2]
     vir_width = regrouped.shape[3]
     energy_i = lax.dynamic_slice_in_dim(occ_energy, lax.axis_index("occ") * occ_width, occ_width)

time: 433 us -> 445 us (1.028)
  local copies, waits for them, and re-layouts: 15.1 us -> 23.3 us
    split x0 -> x1, local copies, waits for them, and re-layouts: none -> 8.82 us  [local(): cells = jnp.split(integrals, lax.axis_size('occ'), axis=2)]
where the time goes in v1:
time: 445 us
  waiting for transfers between devices  355 us (80%)
  matrix products  32.8 us (7%)
  local copies, waits for them, and re-layouts  23.3 us (5%)
  between operations  20.6 us (5%)
  starting transfers between devices  6.75 us (2%)
  other arithmetic  6.4 us (1%)
    psum x1, waiting for transfers between devices, from_root(): return lax.psum(jnp.where(mine, value, jnp.zeros_like(value)), axis)  188 us
    psum x1, waiting for transfers between devices, local(): lax.psum(partial_value.astype(jnp.bfloat16), 'aux').astype(jnp.float32)  83.1 us
    all_to_all x1, waiting for transfers between devices, local(): received = lax.all_to_all(jnp.stack(cells), 'occ', 0, 0)  57.7 us
    all_gather x2, waiting for transfers between devices, local(): owner_whole = lax.all_gather(owner_half, 'vir', axis=3, tiled=True)  24.9 us
    dot_general x2, matrix products, local(): jnp.einsum('ijab,srjb->sria', amplitude, owner_whole, preferred_element_t...  17.1 us
    dot_general x2, matrix products, local(): jnp.einsum('sria,srjb->ijab', regrouped, owner_whole, preferred_element_t...  15.8 us
    add x1, local copies, waits for them, and re-layouts, local(): gamma_total + jnp.einsum('ijab,srjb->sria', amplitude, owner_whole, prefe...  10.2 us
  transfers between devices with their start and end apart: 5, of which 5 were waited for; matrix products, arithmetic and copies ran while one was open for 2% of the time, Pallas kernels for 0%

profile of v1, /device:TPU:0, one launch (start us, length us, event | category | flops | bytes accessed | tf_op | source)
XLA Modules:
  0.0 444.8 jit_solution(14433480110356045769)
XLA Ops:
  6.5 8.8 %fusion.38 = (bf16[1,512,1,640]{3,2,1,0:T(2,128)(2,1)S(1)}, bf16[1,512,1,640]{3,2,1,0:T(2,128)(2,1)S(1)}, bf16[1,512,1,640]{3,2,1,0:T(2,128)(2,1)S(1)}, bf16[1,512,1,640]{3,2,1,0:T(2,128)(2,1)S(1)}) fusion(bf16[1,512,4,640]{3,2,1,0:T(4,128)(2,1)} %param.4), kind=kLoop, calls=%fused_computation.34 | loop fusion | bytes 5242880 | tf_op jit(solution)/shard_map/split | solution.py:15
  15.4 0.2 copy_bitcast_fusion.2
  15.6 0.2 copy_bitcast_fusion
  15.8 1.9 pad_maximum_fusion
  17.7 0.0 copy-start.2
  17.7 6.4 %all-to-all-start = ((bf16[4,1,512,1,640]{4,2,3,1,0:T(8,128)(2,1)}), bf16[4,1,512,1,640]{4,2,3,1,0:T(8,128)(2,1)S(1)}, u32[]{:S(2)}, u32[]{:S(2)}) async-start(bf16[4,1,512,1,640]{4,2,3,1,0:T(8,128)(2,1)} %pad_maximum_fusion), calls=%async_computation | async-start | bytes 5242880 | tf_op jit(solution)/shard_map/all_to_all | solution.py:16
  24.1 0.0 all-reduce.5.cloned.1.call-start
  24.1 0.0 copy-done.2
  24.1 0.6 fusion.40
  25.9 57.7 %all-to-all-done = bf16[4,1,512,1,640]{4,2,3,1,0:T(8,128)(2,1)S(1)} async-done(((bf16[4,1,512,1,640]{4,2,3,1,0:T(8,128)(2,1)}), bf16[4,1,512,1,640]{4,2,3,1,0:T(8,128)(2,1)S(1)}, u32[]{:S(2)}, u32[]{:S(2)}) %all-to-all-start) | async-done | bytes 2621472 | tf_op jit(solution)/shard_map/all_to_all | solution.py:16
  83.5 2.6 copy.18
  86.1 4.4 select_bitcast_fusion.1
  90.6 0.0 all-reduce.5.cloned.1.call-update
  90.6 0.0 all-gather.3.cloned.1.call-start
  90.7 188.5 %all-reduce.5.cloned.1.call-done = (bf16[4,512,1,640]{1,3,0,2:T(8,128)(2,1)}, bf16[4,512,1,640]{1,3,0,2:T(8,128)(2,1)}) async-done(((bf16[4,512,1,640]{1,3,0,2:T(8,128)(2,1)}, bf16[4,512,1,640]{1,3,0,2:T(8,128)(2,1)}), (bf16[4,512,1,640]{1,3,0,2:T(8,128)(2,1)}, bf16[4,512,1,640]{1,3,0,2:T(8,128)(2,1)})) %all-reduce.5.cloned.1.call-update) | async-done | bytes 5242896 | tf_op jit(solution)/shard_map/psum | solution.py:11
  279.1 0.0 all-gather.3.cloned.1.call-update
  279.2 0.0 all-gather.5.cloned.1.call-start
  279.2 0.7 all-gather.5.cloned.1.call-update
  279.9 0.2 all-reduce.7.cloned.1.call-start
  280.1 14.8 %all-gather.3.cloned.1.call-done = bf16[4,512,1,1280]{1,3,0,2:T(8,128)(2,1)} async-done(((bf16[4,512,1,640]{1,3,0,2:T(8,128)(2,1)}), bf16[4,512,1,1280]{1,3,0,2:T(8,128)(2,1)}) %all-gather.3.cloned.1.call-update) | async-done | bytes 5242896 | tf_op jit(solution)/shard_map/all_gather | solution.py:26
  294.9 7.9 %fusion.20 = bf16[1,1,640,1280]{2,3,0,1:T(8,128)(2,1)} fusion(bf16[4,512,1,1280]{1,3,0,2:T(8,128)(2,1)} %all-gather.3.cloned.1.call-done, bf16[4,1,512,1,640]{4,2,3,1,0:T(8,128)(2,1)S(1)} %all-to-all-done), kind=kOutput, calls=%fused_computation.15 | convolution fusion | flops 3356262400 | bytes 9502720 | tf_op jit(solution)/shard_map/sria,srjb->ijab/dot_general | solution.py:28
  302.8 10.1 %all-gather.5.cloned.1.call-done = bf16[4,512,1,1280]{1,3,0,2:T(8,128)(2,1)} async-done(((bf16[4,512,1,640]{1,3,0,2:T(8,128)(2,1)}), bf16[4,512,1,1280]{1,3,0,2:T(8,128)(2,1)}) %all-gather.5.cloned.1.call-update) | async-done | bytes 5242896 | tf_op jit(solution)/shard_map/all_gather | solution.py:26
  312.9 7.9 %fusion.23 = bf16[1,1,640,1280]{2,3,0,1:T(8,128)(2,1)} fusion(bf16[4,512,1,1280]{1,3,0,2:T(8,128)(2,1)} %all-gather.5.cloned.1.call-done, bf16[4,1,512,1,640]{4,2,3,1,0:T(8,128)(2,1)S(1)} %all-to-all-done), kind=kOutput, calls=%fused_computation.16 | convolution fusion | flops 3356262400 | bytes 9502720 | tf_op jit(solution)/shard_map/sria,srjb->ijab/dot_general | solution.py:28
  320.8 0.0 copy-start
  320.8 0.0 copy-start.1
  320.8 0.0 all-reduce.7.cloned.1.call-update
  324.4 0.0 copy-done
  324.4 0.7 fusion.39
  327.7 0.0 copy-done.1
  327.7 0.1 dynamic-slice_subtract_fusion.1
  327.8 83.1 %all-reduce.7.cloned.1.call-done = (bf16[1,1,640,1280]{2,3,0,1:T(8,128)(2,1)}, bf16[1,1,640,1280]{2,3,0,1:T(8,128)(2,1)}) async-done(((bf16[1,1,640,1280]{2,3,0,1:T(8,128)(2,1)}, bf16[1,1,640,1280]{2,3,0,1:T(8,128)(2,1)}), (bf16[1,1,640,1280]{2,3,0,1:T(8,128)(2,1)}, bf16[1,1,640,1280]{2,3,0,1:T(8,128)(2,1)})) %all-reduce.7.cloned.1.call-update) | async-done | bytes 3276816 | tf_op jit(solution)/shard_map/psum | solution.py:32
  410.9 0.0 copy-start.3
  410.9 7.6 %fusion = f32[4,512,640]{2,1,0:T(8,128)S(1)} fusion(bf16[4,512,1,1280]{1,3,0,2:T(8,128)(2,1)} %all-gather.5.cloned.1.call-done, bf16[1,1,640,1280]{2,3,0,1:T(8,128)(2,1)} %get-tuple-element.7, f32[640]{0:T(1024)S(1)} %get-tuple-element.16, f32[1280]{0:T(1024)S(1)} %copy-done.1), kind=kOutput, calls=%fused_computation | convolution fusion | flops 3358720000 | bytes 12131840 | tf_op jit(solution)/shard_map/ijab,srjb->sria/dot_general | solution.py:34
  418.6 0.0 copy-done.3
  418.6 9.4 %add_bitcast_fusion = f32[4,512,1,640]{3,1,0,2:T(8,128)} fusion(f32[4,512,640]{2,1,0:T(8,128)S(1)} %fusion, bf16[4,512,1,1280]{1,3,0,2:T(8,128)(2,1)} %all-gather.3.cloned.1.call-done, bf16[1,1,640,1280]{2,3,0,1:T(8,128)(2,1)S(1)} %copy-done.3, f32[1280]{0:T(1024)S(1)} %copy-done.1, f32[640]{0:T(1024)S(1)} %get-tuple-element.15), kind=kOutput, calls=%fused_computation.8 | convolution fusion | flops 3360030720 | bytes 17374720 | tf_op jit(solution)/shard_map/ijab,srjb->sria/dot_general | solution.py:34
  428.0 10.2 %copy.24 = f32[4,512,1,640]{3,2,1,0:T(1,128)} copy(f32[4,512,1,640]{3,1,0,2:T(8,128)} %add_bitcast_fusion) | data formatting | bytes 10485760 | tf_op jit(solution)/shard_map/add | solution.py:34
Async XLA Ops:
  17.7 6.5 %copy-start.2 = (s32[2]{0:T(128)S(1)}, s32[2]{0:T(128)}, u32[]{:S(2)}) copy-start(s32[2]{0:T(128)} %param.7) | copy-start | bytes 28
  17.7 65.9 %all-to-all-start = ((bf16[4,1,512,1,640]{4,2,3,1,0:T(8,128)(2,1)}), bf16[4,1,512,1,640]{4,2,3,1,0:T(8,128)(2,1)S(1)}, u32[]{:S(2)}, u32[]{:S(2)}) async-start(bf16[4,1,512,1,640]{4,2,3,1,0:T(8,128)(2,1)} %pad_maximum_fusion), calls=%async_computation | async-start | bytes 5242880 | tf_op jit(solution)/shard_map/all_to_all | solution.py:16
  24.1 255.0 %all-reduce.5.cloned.1.call-start = ((), (), s32[]{:S(2)}) async-start(), calls=%async_computation.3 | async-start | bytes 10485760 | tf_op jit(solution)/shard_map/psum | solution.py:11
  90.6 204.3 %all-gather.3.cloned.1.call-start = ((), (), s32[]{:S(2)}) async-start(), calls=%async_computation.1 | async-start | bytes 7864320 | tf_op jit(solution)/shard_map/all_gather | solution.py:26
  279.2 33.7 %all-gather.5.cloned.1.call-start = ((), (), s32[]{:S(2)}) async-start(), calls=%async_computation.2 | async-start | bytes 7864320 | tf_op jit(solution)/shard_map/all_gather | solution.py:26
  279.9 131.0 %all-reduce.7.cloned.1.call-start = ((), (), s32[]{:S(2)}) async-start(), calls=%async_computation.4 | async-start | bytes 6553600 | tf_op jit(solution)/shard_map/psum | solution.py:32
  320.8 3.6 copy-start
  320.8 6.9 %copy-start.1 = (f32[1280]{0:T(1024)S(1)}, f32[1280]{0:T(1024)}, u32[]{:S(2)}) copy-start(f32[1280]{0:T(1024)} %param.6) | copy-start | bytes 15364
  410.9 7.7 %copy-start.3 = (bf16[1,1,640,1280]{2,3,0,1:T(8,128)(2,1)S(1)}, bf16[1,1,640,1280]{2,3,0,1:T(8,128)(2,1)}, u32[]{:S(2)}) copy-start(bf16[1,1,640,1280]{2,3,0,1:T(8,128)(2,1)} %get-tuple-element.8) | copy-start | bytes 4915204
Sparse Core Ops, SparseCore 0:
  90.7 188.3 all-reduce.4
  280.7 14.1 all-gather.2
  296.5 16.3 all-gather.4
  320.9 89.9 all-reduce.6
